TPU v7x, 32 devices: a whole 2x2x4 slice. The times are simulated.
32 devices in a mesh: row: 4 (over z), col: 4 (over y, x), layer: 2 (over core).
Axes of the slice: x: 2, y: 2, z: 4, core: 2. Of those that a mesh axis runs over, the one named last changes fastest.
Arguments:
- coeffs: bfloat16 [8192, 4096], P('row', 'col'), may hold values from -6 to 6
- block_sizes: int32 [64], P('row'), may hold values from 64 to 128, as said below
- neighbours: int32 [64, 16], P('row'), may hold values from 0 to 63, as said below
- ham_blocks: bfloat16 [64, 16, 128, 128], P('row', 'layer'), may hold values from -0.125 to 0.125
- ovl_blocks: bfloat16 [64, 16, 128, 128], P('row', 'layer'), may hold values from -0.125 to 0.125
Outputs:
- residual: float32 [8192, 4096], P(('row', 'layer'), 'col')
Inputs may be any that keep to these rules, and one draw needn't show every extreme that they name: `block_sizes`: some block has exactly 128 live basis functions. `neighbours`: every entry names a block at most 16 blocks from its row's block; slot 0 names the row's own block.
All inputs are finite; a program needn't handle non-finite values.
Results may differ from a plain program's by a relative error of at most 0.0031.
Values may be sent and summed in bfloat16 or wider, within the bound.
No kernel may reach another device: no remote copies, remote signals or barrier semaphores. Data moves between devices by JAX's collectives and lax.ppermute only.
A program may use at most 128 MiB of HBM per device.

v0:
```python
import jax
import jax.numpy as jnp
from jax import lax
from jax.sharding import PartitionSpec as P


def padded_2(shard, sides, width):
    for axis, dim in sides:
        devices, length = (lax.axis_size(axis), shard.shape[dim])
        up = [(i, (i + 1) % devices) for i in range(devices - 1)]
        down = [(j, i) for i, j in up]
        last = lax.slice_in_dim(shard, length - width, length, axis=dim)
        first = lax.slice_in_dim(shard, 0, width, axis=dim)
        before = lax.ppermute(last, axis, up)
        after = lax.ppermute(first, axis, down)
        shard = jnp.concatenate([before, shard, after], axis=dim)
    return shard


def body(coeffs, block_sizes, neighbours, ham_blocks, ovl_blocks):
    blocks_dev = block_sizes.shape[0]
    block_rows = ham_blocks.shape[2]
    cols_dev = coeffs.shape[1]
    layer_id = lax.axis_index("layer")
    live = jnp.arange(block_rows, dtype=jnp.int32)[None, :] < block_sizes[:, None]
    masked = (
        coeffs.reshape(blocks_dev, block_rows, cols_dev) * live[:, :, None].astype(coeffs.dtype)
    ).reshape(blocks_dev * block_rows, cols_dev)
    padded = padded_2(masked, (("row", 0),), blocks_dev * block_rows)
    padded = padded.reshape(3 * blocks_dev, block_rows, cols_dev)
    first_block = lax.axis_index("row") * blocks_dev - blocks_dev
    live_float = live.astype(jnp.float32)
    half_blocks = blocks_dev // 2
    half_rows = half_blocks * block_rows
    ham_mine, ovl_mine = (
        lax.all_to_all(ham_blocks, "layer", split_axis=0, concat_axis=1, tiled=True),
        lax.all_to_all(ovl_blocks, "layer", split_axis=0, concat_axis=1, tiled=True),
    )
    own_neigh = lax.dynamic_slice_in_dim(neighbours, layer_id * half_blocks, half_blocks, 0)
    own_live = lax.dynamic_slice_in_dim(live_float, layer_id * half_blocks, half_blocks, 0)
    chosen = padded[own_neigh - first_block]
    wpart = (
        jnp.einsum("ikpq,ikqn->ipn", ham_mine, chosen, preferred_element_type=jnp.float32)
        * own_live[:, :, None]
    )
    vpart = (
        jnp.einsum("ikpq,ikqn->ipn", ovl_mine, chosen, preferred_element_type=jnp.float32)
        * own_live[:, :, None]
    )
    hc_half = wpart.reshape(half_rows, cols_dev).astype(jnp.bfloat16)
    sc_half = vpart.reshape(half_rows, cols_dev).astype(jnp.bfloat16)
    masked_half = lax.dynamic_slice_in_dim(masked, layer_id * half_rows, half_rows, 0)
    total_rows = blocks_dev * block_rows * lax.axis_size("row")
    partial_gram = lax.dot_general(
        lax.all_gather(masked_half, "col", axis=1, tiled=True),
        hc_half,
        (((0,), (0,)), ((), ())),
        preferred_element_type=jnp.float32,
    )
    whole_gram = lax.psum(partial_gram, ("row", "layer"))
    gram = (whole_gram / total_rows).astype(jnp.bfloat16)
    projected = jnp.dot(
        lax.all_gather(sc_half, "col", axis=1, tiled=True), gram, preferred_element_type=jnp.float32
    )
    return hc_half.astype(jnp.float32) - projected


def solution(mesh):
    return jax.shard_map(
        body,
        mesh=mesh,
        in_specs=(
            P("row", "col"),
            P("row"),
            P("row", None),
            P("row", "layer", None, None),
            P("row", "layer", None, None),
        ),
        out_specs=P(("row", "layer"), "col"),
        check_vma=False,
    )
```

profile of v0, /device:TPU:0, one launch (start us, length us, event | category | flops | bytes accessed | tf_op | source)
XLA Modules:
  0.0 605.2 jit_solution(4631979231615089417)
XLA Ops:
  6.5 0.0 all-gather.5.cloned.1.call-start
  6.5 0.7 iota_compare_fusion
  7.3 4.5 broadcast_multiply_fusion
  11.8 3.1 constant_dynamic-slice_fusion
  15.0 0.0 all-gather.5.cloned.1.call-update
  15.0 0.0 copy-start.2
  15.0 1.3 collective-permute-start.1
  16.3 7.6 %collective-permute-start = (bf16[2048,1024]{1,0:T(8,128)(2,1)}, bf16[2048,1024]{1,0:T(8,128)(2,1)}, u32[]{:S(2)}, u32[]{:S(2)}) collective-permute-start(bf16[2048,1024]{1,0:T(8,128)(2,1)} %broadcast_multiply_fusion), channel_id=1, source_target_pairs={{0,8},{8,16},{16,24},{1,9},{9,17},{17,25},{2,10},{10,18},{18,26},{... | collective-permute-start | bytes 12582920 | tf_op jit(solution)/shard_map/ppermute | solution.py:14
  23.9 6.0 all-to-all-start.1
  29.8 0.0 all-gather.3.cloned.1.call-start
  29.9 0.0 copy-done.2
  29.9 0.1 reshape.39
  30.0 4.3 all-to-all-done.1
  34.3 0.0 copy-start
  34.3 4.9 copy.7
  39.2 71.6 %collective-permute-done.1 = bf16[2048,1024]{1,0:T(8,128)(2,1)} collective-permute-done((bf16[2048,1024]{1,0:T(8,128)(2,1)}, bf16[2048,1024]{1,0:T(8,128)(2,1)}, u32[]{:S(2)}, u32[]{:S(2)}) %collective-permute-start.1) | collective-permute-done | bytes 4194336 | tf_op jit(solution)/shard_map/ppermute | solution.py:15
  110.8 1.2 collective-permute-done
  112.0 0.0 copy-done
  112.0 10.3 %pad_maximum_fusion = bf16[6144,1024]{1,0:T(8,128)(2,1)} fusion(bf16[2048,1024]{1,0:T(8,128)(2,1)} %collective-permute-done.1, bf16[2048,1024]{1,0:T(8,128)(2,1)S(1)} %copy-done, bf16[2048,1024]{1,0:T(8,128)(2,1)} %collective-permute-done), kind=kLoop, calls=%fused_computation.2 | loop fusion | flops 37748736 | bytes 25165824 | tf_op jit(solution)/shard_map/concatenate | solution.py:16
  122.4 17.2 %gather_fusion = bf16[128,128,1024]{2,1,0:T(8,128)(2,1)} fusion(bf16[48,128,1024]{2,1,0:T(8,128)(2,1)} %bitcast.37, s32[1024]{0:T(1024)S(1)} %pad_clamp_fusion), kind=kCustom, calls=%fused_computation | custom fusion | bytes 67109376 | tf_op jit(solution)/shard_map/gather | solution.py:41
  139.5 15.7 %fusion.2 = bf16[8,1024,128]{1,2,0:T(8,128)(2,1)} fusion(bf16[8,16,128,128]{3,2,1,0:T(8,128)(2,1)} %bitcast.39, bf16[8,16,128,1024]{3,2,1,0:T(8,128)(2,1)} %bitcast.35, f32[8,128]{1,0:T(8,128)S(1)} %dynamic-slice_convert_fusion), kind=kOutput, calls=%fused_computation.6 | convolution fusion | flops 4297064448 | bytes 39849984 | tf_op jit(solution)/shard_map/ikpq,ikqn->ipn/dot_general | solution.py:47
  155.2 0.0 all-gather.3.cloned.1.call-update
  155.2 0.0 all-reduce.2.cloned.1.call-start
  155.3 8.5 %all_to_all.36 = bf16[16,8,128,128]{3,2,1,0:T(8,128)(2,1)S(1)} all-to-all(bf16[16,8,128,128]{3,2,1,0:T(8,128)(2,1)} %param.8), channel_id=1, replica_groups=mesh['row'=4,'col'=4,'layer'=2] {'layer'}, dimensions={0} | all-to-all | bytes 8388608 | tf_op jit(solution)/shard_map/all_to_all | solution.py:36
  163.8 0.3 copy.6
  164.1 16.6 %fusion.3 = bf16[8,1024,128]{1,2,0:T(8,128)(2,1)} fusion(bf16[8,16,128,128]{3,2,1,0:T(8,128)(2,1)S(1)} %bitcast.40, bf16[8,16,128,1024]{3,2,1,0:T(8,128)(2,1)} %bitcast.36, f32[8,128]{1,0:T(8,128)S(1)} %dynamic-slice_convert_fusion), kind=kOutput, calls=%fused_computation.8 | convolution fusion | flops 4297064448 | bytes 39849984 | tf_op jit(solution)/shard_map/ikpq,ikqn->ipn/dot_general | solution.py:43
  180.7 0.0 all-gather.5.cloned.1.call-done
  180.7 16.2 %fusion.5 = f32[4096,1024]{1,0:T(8,128)} fusion(bf16[1024,4096]{1,0:T(8,128)(2,1)} %all-gather.5.cloned.1.call-done, bf16[1024,1024]{1,0:T(8,128)(2,1)} %bitcast.42), kind=kOutput, calls=%fused_computation.18 | convolution fusion | flops 8589934592 | bytes 27262976 | tf_op jit(solution)/shard_map/dot_general | solution.py:54
  196.8 0.0 copy-start.1
  196.8 0.0 all-reduce.2.cloned.1.call-update
  196.9 50.4 %all-gather.3.cloned.1.call-done = bf16[1024,4096]{1,0:T(8,128)(2,1)} async-done(((bf16[1024,1024]{1,0:T(8,128)(2,1)}), bf16[1024,4096]{1,0:T(8,128)(2,1)}) %all-gather.3.cloned.1.call-update) | async-done | bytes 8388624 | tf_op jit(solution)/shard_map/all_gather | solution.py:63
  247.3 335.3 %all-reduce.2.cloned.1.call-done = f32[4096,1024]{1,0:T(8,128)} async-done(((f32[4096,1024]{1,0:T(8,128)}), f32[4096,1024]{1,0:T(8,128)}) %all-reduce.2.cloned.1.call-update) | async-done | bytes 16777232 | tf_op jit(solution)/shard_map/psum | solution.py:60
  582.6 0.0 copy-done.1
  582.6 16.1 %convert_subtract_fusion = f32[1024,1024]{1,0:T(8,128)} fusion(bf16[1024,1024]{1,0:T(8,128)(2,1)S(1)} %bitcast.43, bf16[1024,4096]{1,0:T(8,128)(2,1)} %all-gather.3.cloned.1.call-done, f32[4096,1024]{1,0:T(8,128)} %all-reduce.2.cloned.1.call-done), kind=kOutput, calls=%fused_computation.9 | convolution fusion | flops 8600420352 | bytes 31457280 | tf_op jit(solution)/shard_map/dot_general | solution.py:62
  (3 shorter events, 0.0 us)
Async XLA Ops:
  6.5 174.1 %all-gather.5.cloned.1.call-start = ((), (), s32[]{:S(2)}) async-start(), calls=%async_computation.3 | async-start | bytes 10485760 | tf_op jit(solution)/shard_map/all_gather | solution.py:55
  15.0 14.9 %copy-start.2 = (s32[16,16]{1,0:T(8,128)S(1)}, s32[16,16]{1,0:T(8,128)}, u32[]{:S(2)}) copy-start(s32[16,16]{1,0:T(8,128)} %param.7) | copy-start | bytes 3076
  15.0 95.8 %collective-permute-start.1 = (bf16[2048,1024]{1,0:T(8,128)(2,1)}, bf16[2048,1024]{1,0:T(8,128)(2,1)}, u32[]{:S(2)}, u32[]{:S(2)}) collective-permute-start(bf16[2048,1024]{1,0:T(8,128)(2,1)} %broadcast_multiply_fusion), channel_id=1, source_target_pairs={{8,0},{16,8},{24,16},{9,1},{17,9},{25,17},{10,2},{18,10},{26,18},{... | collective-permute-start | bytes 12582920 | tf_op jit(solution)/shard_map/ppermute | solution.py:15
  16.3 95.7 %collective-permute-start = (bf16[2048,1024]{1,0:T(8,128)(2,1)}, bf16[2048,1024]{1,0:T(8,128)(2,1)}, u32[]{:S(2)}, u32[]{:S(2)}) collective-permute-start(bf16[2048,1024]{1,0:T(8,128)(2,1)} %broadcast_multiply_fusion), channel_id=1, source_target_pairs={{0,8},{8,16},{16,24},{1,9},{9,17},{17,25},{2,10},{10,18},{18,26},{... | collective-permute-start | bytes 12582920 | tf_op jit(solution)/shard_map/ppermute | solution.py:14
  23.9 10.5 %all-to-all-start.1 = ((bf16[16,8,128,128]{3,2,1,0:T(8,128)(2,1)}), bf16[16,8,128,128]{3,2,1,0:T(8,128)(2,1)}, u32[]{:S(2)}, u32[]{:S(2)}) async-start(bf16[16,8,128,128]{3,2,1,0:T(8,128)(2,1)} %param.9), calls=%async_computation.1 | async-start | bytes 8388608 | tf_op jit(solution)/shard_map/all_to_all | solution.py:37
  29.8 217.5 %all-gather.3.cloned.1.call-start = ((), (), s32[]{:S(2)}) async-start(), calls=%async_computation.2 | async-start | bytes 10485760 | tf_op jit(solution)/shard_map/all_gather | solution.py:63
  34.3 77.7 %copy-start = (bf16[2048,1024]{1,0:T(8,128)(2,1)S(1)}, bf16[2048,1024]{1,0:T(8,128)(2,1)}, u32[]{:S(2)}) copy-start(bf16[2048,1024]{1,0:T(8,128)(2,1)} %broadcast_multiply_fusion) | copy-start | bytes 12582916
  155.2 427.4 %all-reduce.2.cloned.1.call-start = ((), (), s32[]{:S(2)}) async-start(), calls=%async_computation.4 | async-start | bytes 33554432 | tf_op jit(solution)/shard_map/psum | solution.py:60
  196.8 385.8 %copy-start.1 = (bf16[8,1024,128]{1,2,0:T(8,128)(2,1)S(1)}, bf16[8,1024,128]{1,2,0:T(8,128)(2,1)}, u32[]{:S(2)}) copy-start(bf16[8,1024,128]{1,2,0:T(8,128)(2,1)} %fusion.3) | copy-start | bytes 6291460
Sparse Core Ops, SparseCore 0:
  15.1 90.1 all-gather.4
  155.4 91.8 all-gather.2
  249.8 332.7 all-reduce.1
where the time goes:
time: 606 us; the launch traced here: 605 us
  waiting for transfers between devices  463 us (76%)
  matrix products  64.5 us (11%)
  local copies, waits for them, and re-layouts  25.6 us (4%)
  other arithmetic  15.6 us (3%)
  starting transfers between devices  14.9 us (2%)
  between operations  13.2 us (2%)
  blocking collectives  8.49 us (1%)
    psum x1, waiting for transfers between devices, body(): whole_gram = lax.psum(partial_gram, ('row', 'layer'))  335 us
    ppermute x1, waiting for transfers between devices, padded_2(): after = lax.ppermute(first, axis, down)  71.6 us
    all_gather x1, waiting for transfers between devices, body(): lax.all_gather(sc_half, 'col', axis=1, tiled=True)  50.4 us
    gather x1, local copies, waits for them, and re-layouts, body(): chosen = padded[own_neigh - first_block]  17.2 us
    dot_general x1, matrix products, body(): jnp.einsum('ikpq,ikqn->ipn', ham_mine, chosen, preferred_element_type=jnp...  16.6 us
    dot_general x1, matrix products, body(): lax.dot_general(lax.all_gather(masked_half, 'col', axis=1, tiled=True), h...  16.2 us
    dot_general x1, matrix products, body(): jnp.dot(lax.all_gather(sc_half, 'col', axis=1, tiled=True), gram, preferr...  16.1 us
    dot_general x1, matrix products, body(): jnp.einsum('ikpq,ikqn->ipn', ovl_mine, chosen, preferred_element_type=jnp...  15.7 us
  transfers between devices with their start and end apart: 6, of which 5 were waited for; matrix products, arithmetic and copies ran while one was open for 13% of the time, Pallas kernels for 0%

commit v1 on v0

v1 whole, which is shorter than its diff:
```python
import jax
import jax.numpy as jnp
from jax import lax
from jax.experimental import pallas as pl
from jax.experimental.pallas import tpu as pltpu
from jax.sharding import PartitionSpec as P

F32 = jnp.float32
BF16 = jnp.bfloat16
SPMM_VMEM = 28 << 20
VMEM = pl.BlockSpec(memory_space=pltpu.VMEM)
SMEM = pl.BlockSpec(memory_space=pltpu.SMEM)
ANY = pl.BlockSpec(memory_space=pl.ANY)


def near(*arrays):
    return [pltpu.with_memory_space_constraint(x, pltpu.VMEM) for x in arrays]


def after(x, *earlier):
    return lax.optimization_barrier((x, *earlier))[0]


def swap(x):
    return lax.ppermute(x, "layer", [(0, 1), (1, 0)])


def split_cols():
    cols = lax.axis_size("col")
    first = max(d for d in range(1, cols + 1) if cols % d == 0 and d * d <= cols)
    return first, cols // first


def shift_first(x, step):
    first, second = split_cols()
    pairs = [(a * second + b, (a + step) % first * second + b) for a in range(first) for b in range(second)]
    return lax.ppermute(x, "col", pairs)


def shift_cross(x, step):
    first, second = split_cols()
    pairs = [
        ((a * second + b) * 2 + c, ((a + step) % first * second + b) * 2 + 1 - c)
        for a in range(first)
        for b in range(second)
        for c in range(2)
    ]
    return lax.ppermute(x, ("col", "layer"), pairs)


def shift_second(x, step):
    first, second = split_cols()
    pairs = [(a * second + b, a * second + (b + step) % second) for a in range(first) for b in range(second)]
    return lax.ppermute(x, "col", pairs)


def plus(a, b):
    return (a.astype(F32) + b.astype(F32)).astype(BF16)


def spmm(where, sizes, layer, own, before, behind, mats, earlier):
    blocks, slots, depth, _ = mats[0].shape
    rows, cols = own.shape
    past = earlier[0].shape[0] if earlier else 0

    def kernel(where, sizes, layer, own, before, behind, ham_a, ham_b, ovl_a, ovl_b, *refs):
        old, (hc, keep, give_s, give_h, held, *mats, sems, arrived) = refs[:-11], refs[-11:]
        half = blocks // 2
        me = layer[0]
        copies = [
            pltpu.make_async_copy(src, held.at[pl.ds(n * blocks, blocks)], sems.at[n])
            for n, src in enumerate((own, before, behind))
        ]
        for copy in copies:
            copy.start()

        def fetch(row):
            pairs = zip((ham_a, ham_b, ovl_a, ovl_b), mats)
            return [
                pltpu.make_async_copy(src.at[row], dst.at[row], arrived.at[n, row]) for n, (src, dst) in enumerate(pairs)
            ]

        def order(n):
            return me * half + n, (1 - me) * half + n

        def begin(n, carry):
            for row in order(n):
                for copy in fetch(row):
                    copy.start()
            return carry

        lax.fori_loop(0, half, begin, 0)
        for copy in copies:
            copy.wait()
        ham_near, ham_far, ovl_near, ovl_far = mats
        for src, dst in zip(old, (keep, give_s, give_h)):
            dst[:past] = src[...]

        def product(row):
            for copy in fetch(row):
                copy.wait()
            both = None
            for k in range(0, 2 * slots, 2):
                pair = (ham_near, ovl_near) if k < slots else (ham_far, ovl_far)
                left = jnp.concatenate(
                    [jnp.concatenate([m[row, k % slots], m[row, k % slots + 1]], axis=1) for m in pair], axis=0
                )
                right = jnp.concatenate([held[where[row, k]], held[where[row, k + 1]]], axis=0)
                one = jnp.dot(left, right, preferred_element_type=F32)
                both = one if both is None else both + one
            alive = lax.broadcasted_iota(jnp.int32, (depth, 1), 0) < sizes[row]
            h, s = (jnp.where(alive, x, 0.0).astype(BF16) for x in (both[:depth], both[depth:]))
            hc[pl.ds(pl.multiple_of(row * depth, depth), depth), :] = h
            return h, s

        def step(n, carry):
            at = pl.ds(pl.multiple_of(n * depth, depth), depth)
            first, second = order(n)
            _, s = product(first)
            keep[past, at, :] = s
            h, s = product(second)
            give_s[past, at, :] = s
            give_h[past, at, :] = h
            return carry

        lax.fori_loop(0, half, step, 0)

    shaped = [x.reshape(blocks, depth, cols) for x in (own, before, behind)]
    return pl.pallas_call(
        kernel,
        out_shape=[jax.ShapeDtypeStruct((rows, cols), BF16)]
        + [jax.ShapeDtypeStruct((past + 1, rows // 2, cols), BF16)] * 3,
        in_specs=[SMEM] * 3 + [ANY] * 7 + [VMEM] * len(earlier),
        out_specs=[VMEM] * 4,
        scratch_shapes=[pltpu.VMEM((3 * blocks, depth, cols), BF16)]
        + [pltpu.VMEM(m.shape, BF16) for m in mats]
        + [pltpu.SemaphoreType.DMA((3,)), pltpu.SemaphoreType.DMA((4, blocks))],
        compiler_params=pltpu.CompilerParams(vmem_limit_bytes=SPMM_VMEM),
        cost_estimate=pl.CostEstimate(
            flops=8 * rows * slots * depth * cols,
            bytes_accessed=8 * blocks * slots * depth * depth + 10 * rows * cols,
            transcendentals=0,
        ),
        name="spmm",
    )(where, sizes, layer, *shaped, *mats, *near(*earlier))


def gram(total_rows, layer, lefts, right):
    rows, cols = right.shape
    wide = lefts[0].shape[1]
    tile = min(256, wide)

    def kernel(layer, *refs):
        *lefts, right, out = refs
        for a in range(0, wide, tile):
            total = None
            for n, left in enumerate(lefts):
                size = left.shape[0]
                which = layer[0] if n == 0 else 1 - layer[0]
                some = right[...] if size == rows else right[pl.ds(pl.multiple_of(which * size, size), size), :]
                one = lax.dot_general(
                    left[:, a : a + tile], some, (((0,), (0,)), ((), ())), preferred_element_type=F32
                )
                total = one if total is None else total + one
            out[a : a + tile, :] = (total * (1.0 / total_rows)).astype(BF16)

    return pl.pallas_call(
        kernel,
        out_shape=jax.ShapeDtypeStruct((wide, cols), BF16),
        in_specs=[SMEM] + [VMEM] * (len(lefts) + 1),
        out_specs=VMEM,
        compiler_params=pltpu.CompilerParams(vmem_limit_bytes=8 << 20),
        cost_estimate=pl.CostEstimate(
            flops=2 * rows * wide * cols, bytes_accessed=2 * rows * (wide + cols), transcendentals=0
        ),
        name="gram",
    )(layer, *near(*lefts, right))


def product(layer, stacks, grams, tile, put):
    chunks, half, piece = stacks[0].shape
    for r in range(0, half, tile):
        totals = [None, None]
        for n, stack in enumerate(stacks):
            which = layer if n % 2 == 0 else 1 - layer
            for j in range(chunks):
                at = pl.ds(pl.multiple_of(which * (chunks * piece) + j * piece, piece), piece)
                left = stack[j, r : r + tile, :]
                for c in range(2):
                    one = jnp.dot(left, grams[n // 2][c][at, :], preferred_element_type=F32)
                    totals[c] = one if totals[c] is None else totals[c] + one
        put(r, totals)


def foreign(layer, stacks, grams):
    _, half, piece = stacks[0].shape
    tile = min(256, half)
    count = len(stacks)

    def kernel(layer, *refs):
        stacks, pairs, out = refs[:count], refs[count:-1], refs[-1]

        def put(r, totals):
            for c in range(2):
                out[r : r + tile, c * piece : (c + 1) * piece] = totals[c].astype(BF16)

        product(layer[0], stacks, list(zip(pairs[::2], pairs[1::2])), tile, put)

    return pl.pallas_call(
        kernel,
        out_shape=jax.ShapeDtypeStruct((half, 2 * piece), BF16),
        in_specs=[SMEM] + [VMEM] * (2 * count),
        out_specs=VMEM,
        compiler_params=pltpu.CompilerParams(vmem_limit_bytes=8 << 20),
        name="foreign",
    )(layer, *near(*stacks, *[g for pair in grams for g in pair]))


def finish(layer, j, stacks, grams, hc, hc_other, got, out):
    chunks, half, piece = stacks[0].shape
    width = chunks * piece
    tile = min(256, half)
    steps = half // tile
    count, others = len(stacks), len(got)

    def kernel(layer, *refs):
        stacks, pairs = refs[:count], refs[count : 2 * count]
        hc, hc_other = refs[2 * count], refs[2 * count + 1]
        got = refs[2 * count + 2 : 2 * count + 2 + others]
        out, made, sems = refs[-3:]
        me = layer[0]
        copies = []

        def put(r, totals):
            for c in range(2):
                if c == 0:
                    mine = hc[pl.ds(pl.multiple_of(me * half + r, tile), tile), :]
                else:
                    mine = hc_other[j, r : r + tile, :]
                value = mine.astype(F32) - totals[c]
                for g in got:
                    value = value - g[r : r + tile, c * piece : (c + 1) * piece].astype(F32)
                made[c, r : r + tile, :] = value
                which = me if c == 0 else 1 - me
                at = pl.ds(pl.multiple_of(which * width + j * piece, piece), piece)
                copy = pltpu.make_async_copy(
                    made.at[c, pl.ds(r, tile), :], out.at[pl.ds(r, tile), at], sems.at[c, r // tile]
                )
                copy.start()
                copies.append(copy)

        product(me, stacks, list(zip(pairs[::2], pairs[1::2])), tile, put)
        for copy in copies:
            copy.wait()

    operands = [layer, *near(*stacks, *[g for pair in grams for g in pair], hc, hc_other, *got)]
    specs = [SMEM] + [VMEM] * (len(operands) - 1)
    alias = {}
    if out is not None:
        alias = {len(operands): 0}
        operands.append(out)
        specs.append(ANY)
    return pl.pallas_call(
        kernel,
        out_shape=jax.ShapeDtypeStruct((half, 2 * width), F32),
        in_specs=specs,
        out_specs=ANY,
        scratch_shapes=[pltpu.VMEM((2, half, piece), F32), pltpu.SemaphoreType.DMA((2, steps))],
        input_output_aliases=alias,
        compiler_params=pltpu.CompilerParams(vmem_limit_bytes=8 << 20),
        name="finish",
    )(*operands)


def body(coeffs, block_sizes, neighbours, ham_blocks, ovl_blocks):
    blocks, slots, depth, _ = ham_blocks.shape
    rows, cols = coeffs.shape
    devices = lax.axis_size("row")
    first, second = split_cols()
    row_id, layer_id = lax.axis_index("row"), lax.axis_index("layer")
    layer = layer_id.reshape(1).astype(jnp.int32)
    width = cols // 2
    chunks = 2 if width % 256 == 0 else 1
    piece = width // chunks
    half = rows // 2
    middle = devices // 2

    live = jnp.arange(depth, dtype=jnp.int32)[None, :] < block_sizes[:, None]
    mask = live.reshape(rows, 1).astype(coeffs.dtype)
    mine = [
        lax.dynamic_slice_in_dim(coeffs, layer_id * width + j * piece, piece, 1) * mask for j in range(chunks)
    ]
    up = [(i, i + 1) for i in range(devices - 1)]
    down = [(j, i) for i, j in up]
    halo = []
    for j, x in enumerate(mine):
        before = lax.ppermute(x, "row", up)
        behind = lax.ppermute(x, "row", down)
        halo.append((before, behind))
    raw = lax.dynamic_slice_in_dim(after(coeffs, *mine), layer_id * half, half, 0)
    sides = [shift_first(raw, step) for step in range(1, first)]
    ham_other, ovl_other = swap(after(ham_blocks, *mine)), swap(after(ovl_blocks, *mine))
    mats = (ham_blocks, ham_other, ovl_blocks, ovl_other)

    where = neighbours - row_id * blocks
    where = jnp.where(where < 0, where + 2 * blocks, jnp.where(where >= blocks, where + blocks, where))
    where = jnp.where(layer_id == 0, where, jnp.roll(where, slots, axis=1))

    hcs, joined, token = [], [], None
    lefts = [[coeffs]]
    groups = []
    for j in range(chunks):
        there = list(range(1, second))
        groups += [(j, s) for s in ([0] + there if j < chunks - 1 else there + [0])]
    order = [(j, s, t) for j, s in groups for t in range(first)]
    value = {}
    flight = {}

    stages = []
    for t in range(middle - 1):
        stages.append(([(t, t + 1), (devices - 1 - t, devices - 2 - t)], None))
    if devices > 1:
        stages.append(([(middle - 1, middle), (middle, middle - 1)], None))
    for t in reversed(range(middle - 1)):
        stages.append(([(t + 1, t), (devices - 2 - t, devices - 1 - t)], (row_id == t) | (row_id == devices - 1 - t)))

    def launch(n):
        nonlocal token
        j, s, t = order[n]
        right = hcs[j][s] if token is None else after(hcs[j][s], token)
        token = value[n] = gram(rows * devices, layer, lefts[t], right)
        if stages:
            flight[n] = lax.ppermute(value[n], "row", stages[0][0])

    for j in range(chunks):
        x, (before, behind) = mine[j], halo[j]
        if token is not None:
            x = after(x, token)
        hc, *joined = spmm(where, block_sizes, layer, x, before, behind, mats, joined)
        token = hc
        hcs.append([hc] + [shift_second(hc, s) for s in range(1, second)])
        if j == 0:
            if groups[0] == (0, 0):
                launch(0)
            for got in sides:
                got = after(got, token)
                lefts.append([got, swap(got)])
            if groups[0] == (0, 0):
                for t in range(1, first):
                    launch(t)
    launched = first if groups[0] == (0, 0) else 0

    keep, give_s, give_h = joined
    stacks = [keep, swap(give_s)]
    for step in range(1, first):
        stacks += [shift_first(keep, step), shift_cross(give_s, step)]
    hc_other = swap(give_h)

    depth_of = len(stages)
    ready, done, waiting = {}, {}, []
    out = None
    count = len(order)
    for tick in range(count + depth_of):
        while launched < count and launched <= tick:
            launch(launched)
            launched += 1
        for k in range(depth_of):
            n = tick - k
            if not 0 <= n < count:
                continue
            _, take = stages[k]
            got = after(flight[n], token)
            value[n] = plus(value[n], got) if take is None else jnp.where(take, got, value[n])
            token = value[n]
            if k + 1 < depth_of:
                flight[n] = lax.ppermute(value[n], "row", stages[k + 1][0])
        n = tick - max(depth_of - 1, 0)
        if 0 <= n < count:
            j, s, t = order[n]
            ready[j, s, t] = (value[n], swap(value[n]))
            if t == first - 1:
                waiting.append((j, s))
        while launched < count and launched <= tick + 2 and tick + 1 < count:
            launch(launched)
            launched += 1
        for j, s in list(waiting):
            if s == 0 and any((j, m) not in done for m in range(1, second)):
                continue
            grams = [ready[j, s, t] for t in range(first)]
            mine_first = [after(stacks[0], token)] + stacks[1:]
            if s:
                token = foreign(layer, mine_first, grams)
                done[j, s] = shift_second(token, second - s)
            else:
                got = [done[j, m] for m in range(1, second)]
                token = out = finish(layer, j, mine_first, grams, hcs[j][0], hc_other, got, out)
            waiting.remove((j, s))
    return out


def solution(mesh):
    return jax.shard_map(
        body,
        mesh=mesh,
        in_specs=(
            P("row", "col"),
            P("row"),
            P("row", None),
            P("row", "layer", None, None),
            P("row", "layer", None, None),
        ),
        out_specs=P(("row", "layer"), "col"),
        check_vma=False,
    )
```

time: 606 us -> 281 us (0.46)
  the two profiles are of different devices: /device:TPU:0 before, /device:TPU:8 now
where the time goes in v1:
time: 281 us; the launch traced here: 280 us
  waiting for transfers between devices  132 us (47%)
  starting transfers between devices  70.2 us (25%)
  Pallas kernels  58.8 us (21%)
  other arithmetic  9.75 us (3%)
  local copies, waits for them, and re-layouts  8.14 us (3%)
    ppermute x16, waiting for transfers between devices, body(): flight[n] = lax.ppermute(value[n], 'row', stages[k + 1][0])  54.8 us
    ppermute x16, starting transfers between devices, body(): flight[n] = lax.ppermute(value[n], 'row', stages[k + 1][0])  37.4 us
    ppermute x2, waiting for transfers between devices, body(): before = lax.ppermute(x, 'row', up)  33.1 us
    pallas_call x2, Pallas kernels, spmm(): pl.pallas_call(kernel, out_shape=[jax.ShapeDtypeStruct((rows, cols), BF16...  29.7 us
    ppermute x4, waiting for transfers between devices, shift_second(): return lax.ppermute(x, 'col', pairs)  23.5 us
    pallas_call x8, Pallas kernels, gram(): pl.pallas_call(kernel, out_shape=jax.ShapeDtypeStruct((wide, cols), BF16)...  16.6 us
    ppermute x8, waiting for transfers between devices, launch(): flight[n] = lax.ppermute(value[n], 'row', stages[0][0])  15 us
    ppermute x8, starting transfers between devices, launch(): flight[n] = lax.ppermute(value[n], 'row', stages[0][0])  10.3 us
  transfers between devices with their start and end apart: 48, of which 23 were waited for; matrix products, arithmetic and copies ran while one was open for 3% of the time, Pallas kernels for 20%

profile of v1, /device:TPU:8, one launch (start us, length us, event | category | flops | bytes accessed | tf_op | source)
XLA Modules:
  0.0 280.3 jit_solution(7597062641028633396)
XLA Ops:
  0.7 3.0 %dynamic-slice_multiply_fusion = (bf16[2048,256]{1,0:T(8,128)(2,1)}, bf16[2048,256]{1,0:T(8,128)(2,1)S(1)}) fusion(bf16[2048,1024]{1,0:T(8,128)(2,1)} %refs_0_.7, s32[]{:T(128)S(6)} %select_n.65, bf16[2048]{0:T(1024)(128)(2,1)S(1)} %fusion.2, s32[]{:T(128)S(6)} %select_n.64), kind=kLoop, calls=%fused_computation.16 | loop fusion | flops 3670016 | bytes 4198408 | tf_op jit(solution)/shard_map/mul | solution.py:291
  4.3 3.1 %constant_dynamic-slice_fusion = bf16[1024,1024]{1,0:T(8,128)(2,1)} fusion(bf16[2048,1024]{1,0:T(8,128)(2,1)} %refs_0_.7, s32[]{:T(128)S(6)} %select_n.66), kind=kLoop, calls=%fused_computation.32 | loop fusion | bytes 4194308 | tf_op jit(solution)/shard_map/dynamic_slice | solution.py:300
  8.8 3.5 %collective-permute-start.1 = (bf16[2048,256]{1,0:T(8,128)(2,1)}, bf16[2048,256]{1,0:T(8,128)(2,1)}, u32[]{:S(2)}, u32[]{:S(2)}) collective-permute-start(bf16[2048,256]{1,0:T(8,128)(2,1)} %get-tuple-element.103), channel_id=1, source_target_pairs={{0,8},{8,16},{16,24},{1,9},{9,17},{17,25},{2,10},{10,18},{18,26},{... | collective-permute-start | bytes 3145736 | tf_op jit(solution)/shard_map/ppermute | solution.py:297
  12.3 3.4 %collective-permute-start.2 = (bf16[2048,256]{1,0:T(8,128)(2,1)}, bf16[2048,256]{1,0:T(8,128)(2,1)}, u32[]{:S(2)}, u32[]{:S(2)}) collective-permute-start(bf16[2048,256]{1,0:T(8,128)(2,1)} %get-tuple-element.103), channel_id=1, source_target_pairs={{8,0},{16,8},{24,16},{9,1},{17,9},{25,17},{10,2},{18,10},{26,18},{... | collective-permute-start | bytes 3145736 | tf_op jit(solution)/shard_map/ppermute | solution.py:298
  15.9 19.9 %collective-permute-done.1 = bf16[2048,256]{1,0:T(8,128)(2,1)} collective-permute-done((bf16[2048,256]{1,0:T(8,128)(2,1)}, bf16[2048,256]{1,0:T(8,128)(2,1)}, u32[]{:S(2)}, u32[]{:S(2)}) %collective-permute-start.1) | collective-permute-done | bytes 1048608 | tf_op jit(solution)/shard_map/ppermute | solution.py:297
  35.8 3.2 %collective-permute-done.2 = bf16[2048,256]{1,0:T(8,128)(2,1)} collective-permute-done((bf16[2048,256]{1,0:T(8,128)(2,1)}, bf16[2048,256]{1,0:T(8,128)(2,1)}, u32[]{:S(2)}, u32[]{:S(2)}) %collective-permute-start.2) | collective-permute-done | bytes 1048608 | tf_op jit(solution)/shard_map/ppermute | solution.py:298
  39.1 15.8 %spmm.2 = (bf16[2048,256]{1,0:T(8,128)(2,1)}, bf16[1,1024,256]{2,1,0:T(8,128)(2,1)S(1)}, bf16[1,1024,256]{2,1,0:T(8,128)(2,1)S(1)}, bf16[1,1024,256]{2,1,0:T(8,128)(2,1)S(1)}) custom-call(s32[16,16]{1,0:T(8,128)S(1)} %add_select_fusion.where, s32[16]{0:T(128)S(1)} %copy-done.9, s32[1]{0:T(128)} %bitcast.layer, bf16[16,128,256]{2,1,0:T(8,128)(2,1)} %bitcast.2.own, ...), custom_call_target="tpu_custom_call" | custom-call | flops 4294967296 | bytes 22020096 | tf_op jit(solution)/shard_map/spmm/pallas_call | solution.py:129
  54.9 2.5 gram.8
  57.6 3.5 %collective-permute-start.6 = (bf16[2048,256]{1,0:T(8,128)(2,1)S(1)}, bf16[2048,256]{1,0:T(8,128)(2,1)S(1)}, u32[]{:S(2)}, u32[]{:S(2)}) collective-permute-start(bf16[2048,256]{1,0:T(8,128)(2,1)S(1)} %get-tuple-element.61), channel_id=1, source_target_pairs={{0,8},{8,16},{16,24},{1,9},{9,17},{17,25},{2,10},{10,18},{18,26},{... | collective-permute-start | bytes 3145736 | tf_op jit(solution)/shard_map/ppermute | solution.py:297
  61.1 2.4 collective-permute-start.7
  66.4 3.4 %gram.9 = bf16[1024,256]{1,0:T(8,128)(2,1)} custom-call(s32[1]{0:T(128)} %bitcast.layer, bf16[1024,1024]{1,0:T(8,128)(2,1)S(1)} %collective-permute-done.refs_0_, bf16[1024,1024]{1,0:T(8,128)(2,1)S(1)} %collective-permute-done.5.refs_1_, bf16[2048,256]{1,0:T(8,128)(2,1)} %get-tuple-element.60.refs_1_.refs_2_.refs_8_), custom_call_target="tpu_custom_call" | custom-call | flops 1073741824 | bytes 5242880 | tf_op jit(solution)/shard_map/gram/pallas_call | solution.py:167
  72.3 13.1 %collective-permute-done.6 = bf16[2048,256]{1,0:T(8,128)(2,1)S(1)} collective-permute-done((bf16[2048,256]{1,0:T(8,128)(2,1)S(1)}, bf16[2048,256]{1,0:T(8,128)(2,1)S(1)}, u32[]{:S(2)}, u32[]{:S(2)}) %collective-permute-start.6) | collective-permute-done | bytes 1048608 | tf_op jit(solution)/shard_map/ppermute | solution.py:297
  85.5 2.7 collective-permute-done.7
  88.2 13.8 %spmm.3 = (bf16[2048,256]{1,0:T(8,128)(2,1)S(1)}, bf16[2,1024,256]{2,1,0:T(8,128)(2,1)S(1)}, bf16[2,1024,256]{2,1,0:T(8,128)(2,1)S(1)}, bf16[2,1024,256]{2,1,0:T(8,128)(2,1)S(1)}) custom-call(s32[16,16]{1,0:T(8,128)S(1)} %add_select_fusion.where, s32[16]{0:T(128)S(1)} %copy-done.9, s32[1]{0:T(128)} %bitcast.layer, bf16[16,128,256]{2,1,0:T(8,128)(2,1)S(1)} %bitcast.9, ...), custom_call_target="tpu_custom_call" | custom-call | flops 4294967296 | bytes 22020096 | tf_op jit(solution)/shard_map/spmm/pallas_call | solution.py:129
  104.6 2.7 collective-permute-start.10
  109.5 2.2 copy-done.1
  111.7 2.7 gram.10
  117.1 3.0 %collective-permute-done.10 = bf16[1024,256]{1,0:T(8,128)(2,1)} collective-permute-done((bf16[1024,256]{1,0:T(8,128)(2,1)}, bf16[1024,256]{1,0:T(8,128)(2,1)}, u32[]{:S(2)}, u32[]{:S(2)}) %collective-permute-start.10) | collective-permute-done | bytes 524320 | tf_op jit(solution)/shard_map/ppermute | solution.py:376
  120.1 2.5 collective-permute-start.15
  123.9 2.7 gram.11
  126.6 3.6 %collective-permute-done.16 = bf16[1024,256]{1,0:T(8,128)(2,1)S(1)} collective-permute-done((bf16[1024,256]{1,0:T(8,128)(2,1)S(1)}, bf16[1024,256]{1,0:T(8,128)(2,1)S(1)}, u32[]{:S(2)}, u32[]{:S(2)}) %collective-permute-start.16) | collective-permute-done | bytes 524320 | tf_op jit(solution)/shard_map/ppermute | solution.py:333
  131.8 2.6 collective-permute-done.15
  135.8 6.4 %collective-permute-done.14 = bf16[1024,256]{1,0:T(8,128)(2,1)S(1)} collective-permute-done((bf16[1024,256]{1,0:T(8,128)(2,1)S(1)}, bf16[1024,256]{1,0:T(8,128)(2,1)S(1)}, u32[]{:S(2)}, u32[]{:S(2)}) %collective-permute-start.14) | collective-permute-done | bytes 524320 | tf_op jit(solution)/shard_map/ppermute | solution.py:376
  142.2 3.2 %collective-permute-start.20 = (bf16[1024,256]{1,0:T(8,128)(2,1)S(1)}, bf16[1024,256]{1,0:T(8,128)(2,1)S(1)}, u32[]{:S(2)}, u32[]{:S(2)}) collective-permute-start(bf16[1024,256]{1,0:T(8,128)(2,1)S(1)} %add_convert_fusion.12), channel_id=1, source_target_pairs={{8,16},{16,8},{9,17},{17,9},{10,18},{18,10},{11,19},{19,11},{12,20... | collective-permute-start | bytes 1572872 | tf_op jit(solution)/shard_map/ppermute | solution.py:376
  148.5 1.9 collective-permute-start.19
  150.6 5.8 %collective-permute-done.20 = bf16[1024,256]{1,0:T(8,128)(2,1)S(1)} collective-permute-done((bf16[1024,256]{1,0:T(8,128)(2,1)S(1)}, bf16[1024,256]{1,0:T(8,128)(2,1)S(1)}, u32[]{:S(2)}, u32[]{:S(2)}) %collective-permute-start.20) | collective-permute-done | bytes 524320 | tf_op jit(solution)/shard_map/ppermute | solution.py:376
  157.8 2.1 collective-permute-done.19
  159.8 3.2 %collective-permute-start.17 = (bf16[1024,256]{1,0:T(8,128)(2,1)S(1)}, bf16[1024,256]{1,0:T(8,128)(2,1)S(1)}, u32[]{:S(2)}, u32[]{:S(2)}) collective-permute-start(bf16[1024,256]{1,0:T(8,128)(2,1)S(1)} %add_convert_fusion.10), channel_id=1, source_target_pairs={{8,16},{16,8},{9,17},{17,9},{10,18},{18,10},{11,19},{19,11},{12,20... | collective-permute-start | bytes 1572872 | tf_op jit(solution)/shard_map/ppermute | solution.py:376
  164.4 5.2 %collective-permute-done.18 = bf16[1024,256]{1,0:T(8,128)(2,1)S(1)} collective-permute-done((bf16[1024,256]{1,0:T(8,128)(2,1)S(1)}, bf16[1024,256]{1,0:T(8,128)(2,1)S(1)}, u32[]{:S(2)}, u32[]{:S(2)}) %collective-permute-start.18) | collective-permute-done | bytes 524320 | tf_op jit(solution)/shard_map/ppermute | solution.py:333
  171.2 1.6 collective-permute-done.17
  174.2 4.9 %collective-permute-done.24 = bf16[1024,256]{1,0:T(8,128)(2,1)S(1)} collective-permute-done((bf16[1024,256]{1,0:T(8,128)(2,1)S(1)}, bf16[1024,256]{1,0:T(8,128)(2,1)S(1)}, u32[]{:S(2)}, u32[]{:S(2)}) %collective-permute-start.24) | collective-permute-done | bytes 524320 | tf_op jit(solution)/shard_map/ppermute | solution.py:376
  179.2 3.1 %collective-permute-start.22 = (bf16[1024,256]{1,0:T(8,128)(2,1)S(1)}, bf16[1024,256]{1,0:T(8,128)(2,1)S(1)}, u32[]{:S(2)}, u32[]{:S(2)}) collective-permute-start(bf16[1024,256]{1,0:T(8,128)(2,1)S(1)} %add_convert_fusion.8), channel_id=1, source_target_pairs={{8,16},{16,8},{9,17},{17,9},{10,18},{18,10},{11,19},{19,11},{12,20... | collective-permute-start | bytes 1572872 | tf_op jit(solution)/shard_map/ppermute | solution.py:376
  186.6 4.3 %collective-permute-done.22 = bf16[1024,256]{1,0:T(8,128)(2,1)S(1)} collective-permute-done((bf16[1024,256]{1,0:T(8,128)(2,1)S(1)}, bf16[1024,256]{1,0:T(8,128)(2,1)S(1)}, u32[]{:S(2)}, u32[]{:S(2)}) %collective-permute-start.22) | collective-permute-done | bytes 524320 | tf_op jit(solution)/shard_map/ppermute | solution.py:376
  191.0 2.4 collective-permute-done.21
  195.4 3.2 %collective-permute-start.27 = (bf16[1024,256]{1,0:T(8,128)(2,1)S(1)}, bf16[1024,256]{1,0:T(8,128)(2,1)S(1)}, u32[]{:S(2)}, u32[]{:S(2)}) collective-permute-start(bf16[1024,256]{1,0:T(8,128)(2,1)S(1)} %add_convert_fusion.6), channel_id=1, source_target_pairs={{8,16},{16,8},{9,17},{17,9},{10,18},{18,10},{11,19},{19,11},{12,20... | collective-permute-start | bytes 1572872 | tf_op jit(solution)/shard_map/ppermute | solution.py:376
  198.6 1.9 collective-permute-start.26
  201.9 2.3 foreign.2
  204.9 5.0 %collective-permute-done.28 = bf16[1024,256]{1,0:T(8,128)(2,1)S(1)} collective-permute-done((bf16[1024,256]{1,0:T(8,128)(2,1)S(1)}, bf16[1024,256]{1,0:T(8,128)(2,1)S(1)}, u32[]{:S(2)}, u32[]{:S(2)}) %collective-permute-start.28) | collective-permute-done | bytes 524320 | tf_op jit(solution)/shard_map/ppermute | solution.py:333
  213.5 3.2 %collective-permute-start.40 = (bf16[1024,256]{1,0:T(8,128)(2,1)S(1)}, bf16[1024,256]{1,0:T(8,128)(2,1)S(1)}, u32[]{:S(2)}, u32[]{:S(2)}) collective-permute-start(bf16[1024,256]{1,0:T(8,128)(2,1)S(1)} %add_convert_fusion.4), channel_id=1, source_target_pairs={{8,16},{16,8},{9,17},{17,9},{10,18},{18,10},{11,19},{19,11},{12,20... | collective-permute-start | bytes 1572872 | tf_op jit(solution)/shard_map/ppermute | solution.py:376
  216.8 2.3 collective-permute-start.39
  219.2 10.1 %collective-permute-done.37.refs_10_ = bf16[1024,512]{1,0:T(8,128)(2,1)S(1)} collective-permute-done((bf16[1024,512]{1,0:T(8,128)(2,1)S(1)}, bf16[1024,512]{1,0:T(8,128)(2,1)S(1)}, u32[]{:S(2)}, u32[]{:S(2)}) %collective-permute-start.37) | collective-permute-done | bytes 1048608 | tf_op jit(solution)/shard_map/ppermute | solution.py:54
  229.3 4.6 %finish.2.refs_11_ = f32[1024,1024]{1,0:T(8,128)} custom-call(s32[1]{0:T(128)} %bitcast.layer, bf16[2,1024,256]{2,1,0:T(8,128)(2,1)S(1)} %get-tuple-element.102.refs_0_, bf16[2,1024,256]{2,1,0:T(8,128)(2,1)S(1)} %collective-permute-done.29.refs_1_, bf16[2,1024,256]{2,1,0:T(8,128)(2,1)S(1)} %collective-permute-done.30.refs_2_, ...), custom_call_target="tpu_custom_call" | custom-call | tf_op jit(solution)/shard_map/finish/pallas_call | solution.py:263
  234.3 3.2 %collective-permute-start.38 = (bf16[1024,256]{1,0:T(8,128)(2,1)S(1)}, bf16[1024,256]{1,0:T(8,128)(2,1)S(1)}, u32[]{:S(2)}, u32[]{:S(2)}) collective-permute-start(bf16[1024,256]{1,0:T(8,128)(2,1)S(1)} %add_convert_fusion.2), channel_id=1, source_target_pairs={{8,16},{16,8},{9,17},{17,9},{10,18},{18,10},{11,19},{19,11},{12,20... | collective-permute-start | bytes 1572872 | tf_op jit(solution)/shard_map/ppermute | solution.py:376
  238.9 2.3 foreign.3
  241.2 9.3 %collective-permute-done.38 = bf16[1024,256]{1,0:T(8,128)(2,1)S(1)} collective-permute-done((bf16[1024,256]{1,0:T(8,128)(2,1)S(1)}, bf16[1024,256]{1,0:T(8,128)(2,1)S(1)}, u32[]{:S(2)}, u32[]{:S(2)}) %collective-permute-start.38) | collective-permute-done | bytes 524320 | tf_op jit(solution)/shard_map/ppermute | solution.py:376
  252.8 10.4 %collective-permute-done.43 = bf16[1024,256]{1,0:T(8,128)(2,1)S(1)} collective-permute-done((bf16[1024,256]{1,0:T(8,128)(2,1)S(1)}, bf16[1024,256]{1,0:T(8,128)(2,1)S(1)}, u32[]{:S(2)}, u32[]{:S(2)}) %collective-permute-start.43) | collective-permute-done | bytes 524320 | tf_op jit(solution)/shard_map/ppermute | solution.py:376
  263.4 13.4 %collective-permute-done.47.refs_10_ = bf16[1024,512]{1,0:T(8,128)(2,1)S(1)} collective-permute-done((bf16[1024,512]{1,0:T(8,128)(2,1)S(1)}, bf16[1024,512]{1,0:T(8,128)(2,1)S(1)}, u32[]{:S(2)}, u32[]{:S(2)}) %collective-permute-start.47) | collective-permute-done | bytes 1048608 | tf_op jit(solution)/shard_map/ppermute | solution.py:54
  276.8 3.4 %finish.3 = f32[1024,1024]{1,0:T(8,128)} custom-call(s32[1]{0:T(128)} %bitcast.layer, bf16[2,1024,256]{2,1,0:T(8,128)(2,1)S(1)} %get-tuple-element.102.refs_0_, bf16[2,1024,256]{2,1,0:T(8,128)(2,1)S(1)} %collective-permute-done.29.refs_1_, bf16[2,1024,256]{2,1,0:T(8,128)(2,1)S(1)} %collective-permute-done.30.refs_2_, ...), custom_call_target="tpu_custom_call", output_to_operand_aliasing={{}: (12, {})} | custom-call | tf_op jit(solution)/shard_map/finish/pallas_call | solution.py:263
  (120 shorter events, 45.3 us)
Async XLA Ops:
  3.7 35.3 %collective-permute-start.3 = (bf16[16,8,128,128]{3,2,1,0:T(8,128)(2,1)}, bf16[16,8,128,128]{3,2,1,0:T(8,128)(2,1)}, u32[]{:S(2)}, u32[]{:S(2)}) collective-permute-start(bf16[16,8,128,128]{3,2,1,0:T(8,128)(2,1)} %ham_a.3), channel_id=1, source_target_pairs={{0,1},{1,0},{2,3},{3,2},{4,5},{5,4},{6,7},{7,6},{8,9},{9,8},{10,11... | collective-permute-start | bytes 12582920 | tf_op jit(solution)/shard_map/ppermute | solution.py:25
  3.7 35.3 %collective-permute-start.4 = (bf16[16,8,128,128]{3,2,1,0:T(8,128)(2,1)}, bf16[16,8,128,128]{3,2,1,0:T(8,128)(2,1)}, u32[]{:S(2)}, u32[]{:S(2)}) collective-permute-start(bf16[16,8,128,128]{3,2,1,0:T(8,128)(2,1)} %ovl_a.3), channel_id=1, source_target_pairs={{0,1},{1,0},{2,3},{3,2},{4,5},{5,4},{6,7},{7,6},{8,9},{9,8},{10,11... | collective-permute-start | bytes 12582920 | tf_op jit(solution)/shard_map/ppermute | solution.py:25
  7.3 50.1 %collective-permute-start = (bf16[1024,1024]{1,0:T(8,128)(2,1)}, bf16[1024,1024]{1,0:T(8,128)(2,1)S(1)}, u32[]{:S(2)}, u32[]{:S(2)}) collective-permute-start(bf16[1024,1024]{1,0:T(8,128)(2,1)} %constant_dynamic-slice_fusion), channel_id=1, source_target_pairs={{0,4},{2,6},{4,0},{6,2},{1,5},{3,7},{5,1},{7,3},{8,12},{10,14},{12... | collective-permute-start | bytes 6291464 | tf_op jit(solution)/shard_map/ppermute | solution.py:37
  8.8 27.0 %collective-permute-start.1 = (bf16[2048,256]{1,0:T(8,128)(2,1)}, bf16[2048,256]{1,0:T(8,128)(2,1)}, u32[]{:S(2)}, u32[]{:S(2)}) collective-permute-start(bf16[2048,256]{1,0:T(8,128)(2,1)} %get-tuple-element.103), channel_id=1, source_target_pairs={{0,8},{8,16},{16,24},{1,9},{9,17},{17,25},{2,10},{10,18},{18,26},{... | collective-permute-start | bytes 3145736 | tf_op jit(solution)/shard_map/ppermute | solution.py:297
  12.3 26.7 %collective-permute-start.2 = (bf16[2048,256]{1,0:T(8,128)(2,1)}, bf16[2048,256]{1,0:T(8,128)(2,1)}, u32[]{:S(2)}, u32[]{:S(2)}) collective-permute-start(bf16[2048,256]{1,0:T(8,128)(2,1)} %get-tuple-element.103), channel_id=1, source_target_pairs={{8,0},{16,8},{24,16},{9,1},{17,9},{25,17},{10,2},{18,10},{26,18},{... | collective-permute-start | bytes 3145736 | tf_op jit(solution)/shard_map/ppermute | solution.py:298
  57.5 8.9 %collective-permute-start.5 = (bf16[1024,1024]{1,0:T(8,128)(2,1)S(1)}, bf16[1024,1024]{1,0:T(8,128)(2,1)S(1)}, u32[]{:S(2)}, u32[]{:S(2)}) collective-permute-start(bf16[1024,1024]{1,0:T(8,128)(2,1)S(1)} %collective-permute-done.refs_0_), channel_id=1, source_target_pairs={{0,1},{1,0},{2,3},{3,2},{4,5},{5,4},{6,7},{7,6},{8,9},{9,8},{10,11... | collective-permute-start | bytes 6291464 | tf_op jit(solution)/shard_map/ppermute | solution.py:25
  57.6 27.9 %collective-permute-start.6 = (bf16[2048,256]{1,0:T(8,128)(2,1)S(1)}, bf16[2048,256]{1,0:T(8,128)(2,1)S(1)}, u32[]{:S(2)}, u32[]{:S(2)}) collective-permute-start(bf16[2048,256]{1,0:T(8,128)(2,1)S(1)} %get-tuple-element.61), channel_id=1, source_target_pairs={{0,8},{8,16},{16,24},{1,9},{9,17},{17,25},{2,10},{10,18},{18,26},{... | collective-permute-start | bytes 3145736 | tf_op jit(solution)/shard_map/ppermute | solution.py:297
  61.1 27.2 %collective-permute-start.7 = (bf16[2048,256]{1,0:T(8,128)(2,1)S(1)}, bf16[2048,256]{1,0:T(8,128)(2,1)S(1)}, u32[]{:S(2)}, u32[]{:S(2)}) collective-permute-start(bf16[2048,256]{1,0:T(8,128)(2,1)S(1)} %get-tuple-element.61), channel_id=1, source_target_pairs={{8,0},{16,8},{24,16},{9,1},{17,9},{25,17},{10,2},{18,10},{26,18},{... | collective-permute-start | bytes 3145736 | tf_op jit(solution)/shard_map/ppermute | solution.py:298
  63.5 45.3 %collective-permute-start.8 = (bf16[2048,256]{1,0:T(8,128)(2,1)}, bf16[2048,256]{1,0:T(8,128)(2,1)}, u32[]{:S(2)}, u32[]{:S(2)}) collective-permute-start(bf16[2048,256]{1,0:T(8,128)(2,1)} %get-tuple-element.60.refs_1_.refs_2_.refs_8_), channel_id=1, source_target_pairs={{0,2},{2,0},{4,6},{6,4},{1,3},{3,1},{5,7},{7,5},{8,10},{10,8},{12,... | collective-permute-start | bytes 3145736 | tf_op jit(solution)/shard_map/ppermute | solution.py:54
  65.1 38.0 %collective-permute-start.9 = (bf16[1024,256]{1,0:T(8,128)(2,1)S(1)}, bf16[1024,256]{1,0:T(8,128)(2,1)S(1)}, u32[]{:S(2)}, u32[]{:S(2)}) collective-permute-start(bf16[1024,256]{1,0:T(8,128)(2,1)S(1)} %gram.8), channel_id=1, source_target_pairs={{0,8},{24,16},{1,9},{25,17},{2,10},{26,18},{3,11},{27,19},{4,12},{... | collective-permute-start | bytes 1572872 | tf_op jit(solution)/shard_map/ppermute | solution.py:333
  71.0 43.4 %collective-permute-start.11 = (bf16[1024,256]{1,0:T(8,128)(2,1)}, bf16[1024,256]{1,0:T(8,128)(2,1)}, u32[]{:S(2)}, u32[]{:S(2)}) collective-permute-start(bf16[1024,256]{1,0:T(8,128)(2,1)} %gram.9), channel_id=1, source_target_pairs={{0,8},{24,16},{1,9},{25,17},{2,10},{26,18},{3,11},{27,19},{4,12},{... | collective-permute-start | bytes 1572872 | tf_op jit(solution)/shard_map/ppermute | solution.py:333
  104.6 15.5 %collective-permute-start.10 = (bf16[1024,256]{1,0:T(8,128)(2,1)}, bf16[1024,256]{1,0:T(8,128)(2,1)}, u32[]{:S(2)}, u32[]{:S(2)}) collective-permute-start(bf16[1024,256]{1,0:T(8,128)(2,1)} %add_convert_fusion.15), channel_id=1, source_target_pairs={{8,16},{16,8},{9,17},{17,9},{10,18},{18,10},{11,19},{19,11},{12,20... | collective-permute-start | bytes 1572872 | tf_op jit(solution)/shard_map/ppermute | solution.py:376
  107.3 38.3 %collective-permute-start.13 = (bf16[2048,256]{1,0:T(8,128)(2,1)}, bf16[2048,256]{1,0:T(8,128)(2,1)S(1)}, u32[]{:S(2)}, u32[]{:S(2)}) collective-permute-start(bf16[2048,256]{1,0:T(8,128)(2,1)} %copy-done.5), channel_id=1, source_target_pairs={{0,2},{2,0},{4,6},{6,4},{1,3},{3,1},{5,7},{7,5},{8,10},{10,8},{12,... | collective-permute-start | bytes 3145736 | tf_op jit(solution)/shard_map/ppermute | solution.py:54
  108.8 84.7 %collective-permute-start.29 = (bf16[2,1024,256]{2,1,0:T(8,128)(2,1)}, bf16[2,1024,256]{2,1,0:T(8,128)(2,1)S(1)}, u32[]{:S(2)}, u32[]{:S(2)}) collective-permute-start(bf16[2,1024,256]{2,1,0:T(8,128)(2,1)} %copy-done.12), channel_id=1, source_target_pairs={{0,1},{1,0},{2,3},{3,2},{4,5},{5,4},{6,7},{7,6},{8,9},{9,8},{10,11... | collective-permute-start | bytes 3145736 | tf_op jit(solution)/shard_map/ppermute | solution.py:25
  108.8 86.6 %collective-permute-start.31 = (bf16[2,1024,256]{2,1,0:T(8,128)(2,1)}, bf16[2,1024,256]{2,1,0:T(8,128)(2,1)S(1)}, u32[]{:S(2)}, u32[]{:S(2)}) collective-permute-start(bf16[2,1024,256]{2,1,0:T(8,128)(2,1)} %copy-done.12), channel_id=1, source_target_pairs={{0,5},{1,4},{2,7},{3,6},{4,1},{5,0},{6,3},{7,2},{8,13},{9,12},{10,... | collective-permute-start | bytes 3145736 | tf_op jit(solution)/shard_map/ppermute | solution.py:48
  114.4 15.7 %collective-permute-start.16 = (bf16[1024,256]{1,0:T(8,128)(2,1)S(1)}, bf16[1024,256]{1,0:T(8,128)(2,1)S(1)}, u32[]{:S(2)}, u32[]{:S(2)}) collective-permute-start(bf16[1024,256]{1,0:T(8,128)(2,1)S(1)} %gram.10), channel_id=1, source_target_pairs={{0,8},{24,16},{1,9},{25,17},{2,10},{26,18},{3,11},{27,19},{4,12},{... | collective-permute-start | bytes 1572872 | tf_op jit(solution)/shard_map/ppermute | solution.py:333
  120.1 14.3 %collective-permute-start.15 = (bf16[1024,256]{1,0:T(8,128)(2,1)S(1)}, bf16[1024,256]{1,0:T(8,128)(2,1)S(1)}, u32[]{:S(2)}, u32[]{:S(2)}) collective-permute-start(bf16[1024,256]{1,0:T(8,128)(2,1)S(1)} %add_convert_fusion.14), channel_id=1, source_target_pairs={{8,16},{16,8},{9,17},{17,9},{10,18},{18,10},{11,19},{19,11},{12,20... | collective-permute-start | bytes 1572872 | tf_op jit(solution)/shard_map/ppermute | solution.py:376
  130.2 12.0 %collective-permute-start.14 = (bf16[1024,256]{1,0:T(8,128)(2,1)S(1)}, bf16[1024,256]{1,0:T(8,128)(2,1)S(1)}, u32[]{:S(2)}, u32[]{:S(2)}) collective-permute-start(bf16[1024,256]{1,0:T(8,128)(2,1)S(1)} %add_convert_fusion.13), channel_id=1, source_target_pairs={{8,0},{16,24},{9,1},{17,25},{10,2},{18,26},{11,3},{19,27},{12,4},{... | collective-permute-start | bytes 1572872 | tf_op jit(solution)/shard_map/ppermute | solution.py:376
  134.4 14.1 %collective-permute-start.12 = (bf16[1024,256]{1,0:T(8,128)(2,1)S(1)}, bf16[1024,256]{1,0:T(8,128)(2,1)S(1)}, u32[]{:S(2)}, u32[]{:S(2)}) collective-permute-start(bf16[1024,256]{1,0:T(8,128)(2,1)S(1)} %gram.11), channel_id=1, source_target_pairs={{0,8},{24,16},{1,9},{25,17},{2,10},{26,18},{3,11},{27,19},{4,12},{... | collective-permute-start | bytes 1572872 | tf_op jit(solution)/shard_map/ppermute | solution.py:333
  142.2 14.1 %collective-permute-start.20 = (bf16[1024,256]{1,0:T(8,128)(2,1)S(1)}, bf16[1024,256]{1,0:T(8,128)(2,1)S(1)}, u32[]{:S(2)}, u32[]{:S(2)}) collective-permute-start(bf16[1024,256]{1,0:T(8,128)(2,1)S(1)} %add_convert_fusion.12), channel_id=1, source_target_pairs={{8,16},{16,8},{9,17},{17,9},{10,18},{18,10},{11,19},{19,11},{12,20... | collective-permute-start | bytes 1572872 | tf_op jit(solution)/shard_map/ppermute | solution.py:376
  145.5 49.3 %collective-permute-start.30 = (bf16[2,1024,256]{2,1,0:T(8,128)(2,1)S(1)}, bf16[2,1024,256]{2,1,0:T(8,128)(2,1)S(1)}, u32[]{:S(2)}, u32[]{:S(2)}) collective-permute-start(bf16[2,1024,256]{2,1,0:T(8,128)(2,1)S(1)} %get-tuple-element.102.refs_0_), channel_id=1, source_target_pairs={{0,4},{2,6},{4,0},{6,2},{1,5},{3,7},{5,1},{7,3},{8,12},{10,14},{12... | collective-permute-start | bytes 3145736 | tf_op jit(solution)/shard_map/ppermute | solution.py:37
  148.5 11.4 %collective-permute-start.19 = (bf16[1024,256]{1,0:T(8,128)(2,1)S(1)}, bf16[1024,256]{1,0:T(8,128)(2,1)S(1)}, u32[]{:S(2)}, u32[]{:S(2)}) collective-permute-start(bf16[1024,256]{1,0:T(8,128)(2,1)S(1)} %add_convert_fusion.11), channel_id=1, source_target_pairs={{8,0},{16,24},{9,1},{17,25},{10,2},{18,26},{11,3},{19,27},{12,4},{... | collective-permute-start | bytes 1572872 | tf_op jit(solution)/shard_map/ppermute | solution.py:376
  156.3 13.3 %collective-permute-start.18 = (bf16[1024,256]{1,0:T(8,128)(2,1)S(1)}, bf16[1024,256]{1,0:T(8,128)(2,1)S(1)}, u32[]{:S(2)}, u32[]{:S(2)}) collective-permute-start(bf16[1024,256]{1,0:T(8,128)(2,1)S(1)} %gram.12), channel_id=1, source_target_pairs={{0,8},{24,16},{1,9},{25,17},{2,10},{26,18},{3,11},{27,19},{4,12},{... | collective-permute-start | bytes 1572872 | tf_op jit(solution)/shard_map/ppermute | solution.py:333
  159.8 13.0 %collective-permute-start.17 = (bf16[1024,256]{1,0:T(8,128)(2,1)S(1)}, bf16[1024,256]{1,0:T(8,128)(2,1)S(1)}, u32[]{:S(2)}, u32[]{:S(2)}) collective-permute-start(bf16[1024,256]{1,0:T(8,128)(2,1)S(1)} %add_convert_fusion.10), channel_id=1, source_target_pairs={{8,16},{16,8},{9,17},{17,9},{10,18},{18,10},{11,19},{19,11},{12,20... | collective-permute-start | bytes 1572872 | tf_op jit(solution)/shard_map/ppermute | solution.py:376
  169.6 9.6 %collective-permute-start.24 = (bf16[1024,256]{1,0:T(8,128)(2,1)S(1)}, bf16[1024,256]{1,0:T(8,128)(2,1)S(1)}, u32[]{:S(2)}, u32[]{:S(2)}) collective-permute-start(bf16[1024,256]{1,0:T(8,128)(2,1)S(1)} %add_convert_fusion.9), channel_id=1, source_target_pairs={{8,0},{16,24},{9,1},{17,25},{10,2},{18,26},{11,3},{19,27},{12,4},{... | collective-permute-start | bytes 1572872 | tf_op jit(solution)/shard_map/ppermute | solution.py:376
  172.8 12.1 %collective-permute-start.23 = (bf16[1024,256]{1,0:T(8,128)(2,1)S(1)}, bf16[1024,256]{1,0:T(8,128)(2,1)S(1)}, u32[]{:S(2)}, u32[]{:S(2)}) collective-permute-start(bf16[1024,256]{1,0:T(8,128)(2,1)S(1)} %gram.13), channel_id=1, source_target_pairs={{0,8},{24,16},{1,9},{25,17},{2,10},{26,18},{3,11},{27,19},{4,12},{... | collective-permute-start | bytes 1572872 | tf_op jit(solution)/shard_map/ppermute | solution.py:333
  179.2 11.7 %collective-permute-start.22 = (bf16[1024,256]{1,0:T(8,128)(2,1)S(1)}, bf16[1024,256]{1,0:T(8,128)(2,1)S(1)}, u32[]{:S(2)}, u32[]{:S(2)}) collective-permute-start(bf16[1024,256]{1,0:T(8,128)(2,1)S(1)} %add_convert_fusion.8), channel_id=1, source_target_pairs={{8,16},{16,8},{9,17},{17,9},{10,18},{18,10},{11,19},{19,11},{12,20... | collective-permute-start | bytes 1572872 | tf_op jit(solution)/shard_map/ppermute | solution.py:376
  184.9 8.5 %collective-permute-start.21 = (bf16[1024,256]{1,0:T(8,128)(2,1)S(1)}, bf16[1024,256]{1,0:T(8,128)(2,1)S(1)}, u32[]{:S(2)}, u32[]{:S(2)}) collective-permute-start(bf16[1024,256]{1,0:T(8,128)(2,1)S(1)} %add_convert_fusion.7), channel_id=1, source_target_pairs={{8,0},{16,24},{9,1},{17,25},{10,2},{18,26},{11,3},{19,27},{12,4},{... | collective-permute-start | bytes 1572872 | tf_op jit(solution)/shard_map/ppermute | solution.py:376
  190.9 7.7 %collective-permute-start.32 = (bf16[1024,256]{1,0:T(8,128)(2,1)S(1)}, bf16[1024,256]{1,0:T(8,128)(2,1)S(1)}, u32[]{:S(2)}, u32[]{:S(2)}) collective-permute-start(bf16[1024,256]{1,0:T(8,128)(2,1)S(1)} %broadcast_select_fusion.5.refs_4_), channel_id=1, source_target_pairs={{0,1},{1,0},{2,3},{3,2},{4,5},{5,4},{6,7},{7,6},{8,9},{9,8},{10,11... | collective-permute-start | bytes 1572872 | tf_op jit(solution)/shard_map/ppermute | solution.py:25
  193.5 8.4 %collective-permute-start.33 = (bf16[1024,256]{1,0:T(8,128)(2,1)S(1)}, bf16[1024,256]{1,0:T(8,128)(2,1)S(1)}, u32[]{:S(2)}, u32[]{:S(2)}) collective-permute-start(bf16[1024,256]{1,0:T(8,128)(2,1)S(1)} %broadcast_select_fusion.4.refs_6_), channel_id=1, source_target_pairs={{0,1},{1,0},{2,3},{3,2},{4,5},{5,4},{6,7},{7,6},{8,9},{9,8},{10,11... | collective-permute-start | bytes 1572872 | tf_op jit(solution)/shard_map/ppermute | solution.py:25
  193.5 16.3 %collective-permute-start.28 = (bf16[1024,256]{1,0:T(8,128)(2,1)S(1)}, bf16[1024,256]{1,0:T(8,128)(2,1)S(1)}, u32[]{:S(2)}, u32[]{:S(2)}) collective-permute-start(bf16[1024,256]{1,0:T(8,128)(2,1)S(1)} %gram.14), channel_id=1, source_target_pairs={{0,8},{24,16},{1,9},{25,17},{2,10},{26,18},{3,11},{27,19},{4,12},{... | collective-permute-start | bytes 1572872 | tf_op jit(solution)/shard_map/ppermute | solution.py:333
  194.9 18.6 %collective-permute-start.36 = (bf16[2,1024,256]{2,1,0:T(8,128)(2,1)S(1)}, bf16[2,1024,256]{2,1,0:T(8,128)(2,1)S(1)}, u32[]{:S(2)}, u32[]{:S(2)}) collective-permute-start(bf16[2,1024,256]{2,1,0:T(8,128)(2,1)S(1)} %copy-done.11), channel_id=1, source_target_pairs={{0,1},{1,0},{2,3},{3,2},{4,5},{5,4},{6,7},{7,6},{8,9},{9,8},{10,11... | collective-permute-start | bytes 3145736 | tf_op jit(solution)/shard_map/ppermute | solution.py:25
  195.4 15.7 %collective-permute-start.27 = (bf16[1024,256]{1,0:T(8,128)(2,1)S(1)}, bf16[1024,256]{1,0:T(8,128)(2,1)S(1)}, u32[]{:S(2)}, u32[]{:S(2)}) collective-permute-start(bf16[1024,256]{1,0:T(8,128)(2,1)S(1)} %add_convert_fusion.6), channel_id=1, source_target_pairs={{8,16},{16,8},{9,17},{17,9},{10,18},{18,10},{11,19},{19,11},{12,20... | collective-permute-start | bytes 1572872 | tf_op jit(solution)/shard_map/ppermute | solution.py:376
  198.6 13.4 %collective-permute-start.26 = (bf16[1024,256]{1,0:T(8,128)(2,1)S(1)}, bf16[1024,256]{1,0:T(8,128)(2,1)S(1)}, u32[]{:S(2)}, u32[]{:S(2)}) collective-permute-start(bf16[1024,256]{1,0:T(8,128)(2,1)S(1)} %add_convert_fusion.5), channel_id=1, source_target_pairs={{8,0},{16,24},{9,1},{17,25},{10,2},{18,26},{11,3},{19,27},{12,4},{... | collective-permute-start | bytes 1572872 | tf_op jit(solution)/shard_map/ppermute | solution.py:376
  204.2 25.0 %collective-permute-start.37 = (bf16[1024,512]{1,0:T(8,128)(2,1)S(1)}, bf16[1024,512]{1,0:T(8,128)(2,1)S(1)}, u32[]{:S(2)}, u32[]{:S(2)}) collective-permute-start(bf16[1024,512]{1,0:T(8,128)(2,1)S(1)} %foreign.2), channel_id=1, source_target_pairs={{0,2},{2,0},{4,6},{6,4},{1,3},{3,1},{5,7},{7,5},{8,10},{10,8},{12,... | collective-permute-start | bytes 3145736 | tf_op jit(solution)/shard_map/ppermute | solution.py:54
  209.9 6.9 %collective-permute-start.34 = (bf16[1024,256]{1,0:T(8,128)(2,1)S(1)}, bf16[1024,256]{1,0:T(8,128)(2,1)S(1)}, u32[]{:S(2)}, u32[]{:S(2)}) collective-permute-start(bf16[1024,256]{1,0:T(8,128)(2,1)S(1)} %broadcast_select_fusion.7.refs_4_), channel_id=1, source_target_pairs={{0,1},{1,0},{2,3},{3,2},{4,5},{5,4},{6,7},{7,6},{8,9},{9,8},{10,11... | collective-permute-start | bytes 1572872 | tf_op jit(solution)/shard_map/ppermute | solution.py:25
  211.2 8.0 %collective-permute-start.35 = (bf16[1024,256]{1,0:T(8,128)(2,1)S(1)}, bf16[1024,256]{1,0:T(8,128)(2,1)S(1)}, u32[]{:S(2)}, u32[]{:S(2)}) collective-permute-start(bf16[1024,256]{1,0:T(8,128)(2,1)S(1)} %broadcast_select_fusion.6.refs_6_), channel_id=1, source_target_pairs={{0,1},{1,0},{2,3},{3,2},{4,5},{5,4},{6,7},{7,6},{8,9},{9,8},{10,11... | collective-permute-start | bytes 1572872 | tf_op jit(solution)/shard_map/ppermute | solution.py:25
  212.1 21.8 %collective-permute-start.25 = (bf16[1024,256]{1,0:T(8,128)(2,1)S(1)}, bf16[1024,256]{1,0:T(8,128)(2,1)S(1)}, u32[]{:S(2)}, u32[]{:S(2)}) collective-permute-start(bf16[1024,256]{1,0:T(8,128)(2,1)S(1)} %gram.15), channel_id=1, source_target_pairs={{0,8},{24,16},{1,9},{25,17},{2,10},{26,18},{3,11},{27,19},{4,12},{... | collective-permute-start | bytes 1572872 | tf_op jit(solution)/shard_map/ppermute | solution.py:333
  213.5 20.5 %collective-permute-start.40 = (bf16[1024,256]{1,0:T(8,128)(2,1)S(1)}, bf16[1024,256]{1,0:T(8,128)(2,1)S(1)}, u32[]{:S(2)}, u32[]{:S(2)}) collective-permute-start(bf16[1024,256]{1,0:T(8,128)(2,1)S(1)} %add_convert_fusion.4), channel_id=1, source_target_pairs={{8,16},{16,8},{9,17},{17,9},{10,18},{18,10},{11,19},{19,11},{12,20... | collective-permute-start | bytes 1572872 | tf_op jit(solution)/shard_map/ppermute | solution.py:376
  216.8 17.4 %collective-permute-start.39 = (bf16[1024,256]{1,0:T(8,128)(2,1)S(1)}, bf16[1024,256]{1,0:T(8,128)(2,1)S(1)}, u32[]{:S(2)}, u32[]{:S(2)}) collective-permute-start(bf16[1024,256]{1,0:T(8,128)(2,1)S(1)} %add_convert_fusion.3), channel_id=1, source_target_pairs={{8,0},{16,24},{9,1},{17,25},{10,2},{18,26},{11,3},{19,27},{12,4},{... | collective-permute-start | bytes 1572872 | tf_op jit(solution)/shard_map/ppermute | solution.py:376
  219.1 19.8 %collective-permute-start.41 = (bf16[1024,256]{1,0:T(8,128)(2,1)S(1)}, bf16[1024,256]{1,0:T(8,128)(2,1)S(1)}, u32[]{:S(2)}, u32[]{:S(2)}) collective-permute-start(bf16[1024,256]{1,0:T(8,128)(2,1)S(1)} %broadcast_select_fusion.3.refs_4_), channel_id=1, source_target_pairs={{0,1},{1,0},{2,3},{3,2},{4,5},{5,4},{6,7},{7,6},{8,9},{9,8},{10,11... | collective-permute-start | bytes 1572872 | tf_op jit(solution)/shard_map/ppermute | solution.py:25
  234.3 4.6 %collective-permute-start.42 = (bf16[1024,256]{1,0:T(8,128)(2,1)S(1)}, bf16[1024,256]{1,0:T(8,128)(2,1)S(1)}, u32[]{:S(2)}, u32[]{:S(2)}) collective-permute-start(bf16[1024,256]{1,0:T(8,128)(2,1)S(1)} %broadcast_select_fusion.2.refs_6_), channel_id=1, source_target_pairs={{0,1},{1,0},{2,3},{3,2},{4,5},{5,4},{6,7},{7,6},{8,9},{9,8},{10,11... | collective-permute-start | bytes 1572872 | tf_op jit(solution)/shard_map/ppermute | solution.py:25
  234.3 16.2 %collective-permute-start.38 = (bf16[1024,256]{1,0:T(8,128)(2,1)S(1)}, bf16[1024,256]{1,0:T(8,128)(2,1)S(1)}, u32[]{:S(2)}, u32[]{:S(2)}) collective-permute-start(bf16[1024,256]{1,0:T(8,128)(2,1)S(1)} %add_convert_fusion.2), channel_id=1, source_target_pairs={{8,16},{16,8},{9,17},{17,9},{10,18},{18,10},{11,19},{19,11},{12,20... | collective-permute-start | bytes 1572872 | tf_op jit(solution)/shard_map/ppermute | solution.py:376
  237.5 15.1 %collective-permute-start.44 = (bf16[1024,256]{1,0:T(8,128)(2,1)S(1)}, bf16[1024,256]{1,0:T(8,128)(2,1)S(1)}, u32[]{:S(2)}, u32[]{:S(2)}) collective-permute-start(bf16[1024,256]{1,0:T(8,128)(2,1)S(1)} %add_convert_fusion.1), channel_id=1, source_target_pairs={{8,0},{16,24},{9,1},{17,25},{10,2},{18,26},{11,3},{19,27},{12,4},{... | collective-permute-start | bytes 1572872 | tf_op jit(solution)/shard_map/ppermute | solution.py:376
  250.7 12.5 %collective-permute-start.43 = (bf16[1024,256]{1,0:T(8,128)(2,1)S(1)}, bf16[1024,256]{1,0:T(8,128)(2,1)S(1)}, u32[]{:S(2)}, u32[]{:S(2)}) collective-permute-start(bf16[1024,256]{1,0:T(8,128)(2,1)S(1)} %add_convert_fusion), channel_id=1, source_target_pairs={{8,0},{16,24},{9,1},{17,25},{10,2},{18,26},{11,3},{19,27},{12,4},{... | collective-permute-start | bytes 1572872 | tf_op jit(solution)/shard_map/ppermute | solution.py:376
  252.0 24.8 %collective-permute-start.47 = (bf16[1024,512]{1,0:T(8,128)(2,1)S(1)}, bf16[1024,512]{1,0:T(8,128)(2,1)S(1)}, u32[]{:S(2)}, u32[]{:S(2)}) collective-permute-start(bf16[1024,512]{1,0:T(8,128)(2,1)S(1)} %foreign.3), channel_id=1, source_target_pairs={{0,2},{2,0},{4,6},{6,4},{1,3},{3,1},{5,7},{7,5},{8,10},{10,8},{12,... | collective-permute-start | bytes 3145736 | tf_op jit(solution)/shard_map/ppermute | solution.py:54
  252.7 10.6 %collective-permute-start.45 = (bf16[1024,256]{1,0:T(8,128)(2,1)S(1)}, bf16[1024,256]{1,0:T(8,128)(2,1)S(1)}, u32[]{:S(2)}, u32[]{:S(2)}) collective-permute-start(bf16[1024,256]{1,0:T(8,128)(2,1)S(1)} %broadcast_select_fusion.1.refs_4_), channel_id=1, source_target_pairs={{0,1},{1,0},{2,3},{3,2},{4,5},{5,4},{6,7},{7,6},{8,9},{9,8},{10,11... | collective-permute-start | bytes 1572872 | tf_op jit(solution)/shard_map/ppermute | solution.py:25
  263.3 13.5 %collective-permute-start.46 = (bf16[1024,256]{1,0:T(8,128)(2,1)S(1)}, bf16[1024,256]{1,0:T(8,128)(2,1)S(1)}, u32[]{:S(2)}, u32[]{:S(2)}) collective-permute-start(bf16[1024,256]{1,0:T(8,128)(2,1)S(1)} %broadcast_select_fusion.refs_6_), channel_id=1, source_target_pairs={{0,1},{1,0},{2,3},{3,2},{4,5},{5,4},{6,7},{7,6},{8,9},{9,8},{10,11... | collective-permute-start | bytes 1572872 | tf_op jit(solution)/shard_map/ppermute | solution.py:25
  (14 other events, 225.6 us)
